TPU v7x, 32 devices: a whole 2x2x4 slice. The times are simulated.
32 devices in a mesh: ctx: 4 (over y, x), fsdp: 8 (over z, core).
Axes of the slice: x: 2, y: 2, z: 4, core: 2. Of those that a mesh axis runs over, the one named last changes fastest.
Arguments:
- hidden_in: bfloat16 [8, 1024, 1024], P('fsdp', 'ctx'), may hold values from -60 to 60
- lengths: int32 [8], P('fsdp'), may hold values from 128 to 1024, as said below
- block_of: int32 [8, 8], P('fsdp'), may hold values from 0 to 7, each once within a row
- qkv_weight: bfloat16 [1024, 3072], P('fsdp'), may hold values from -0.1875 to 0.1875
- qv_bias: bfloat16 [2048], P('fsdp'), may hold values from -3 to 3
- out_weight: bfloat16 [1024, 1024], P('fsdp'), may hold values from -1.5 to 1.5
- out_bias: bfloat16 [1024], P('fsdp'), may hold values from -3 to 3
- attn_gain: bfloat16 [1024], P('fsdp'), may hold values from 0.5 to 1.5
- attn_shift: bfloat16 [1024], P('fsdp'), may hold values from -3 to 3
- in_weight: bfloat16 [1024, 4096], P('fsdp'), may hold values from -0.1875 to 0.1875
- in_bias: bfloat16 [4096], P('fsdp'), may hold values from -3 to 3
- down_weight: bfloat16 [4096, 1024], P('fsdp'), may hold values from -0.09375 to 0.09375
- down_bias: bfloat16 [1024], P('fsdp'), may hold values from -3 to 3
- ffn_gain: bfloat16 [1024], P('fsdp'), may hold values from 0.5 to 1.5
- ffn_shift: bfloat16 [1024], P('fsdp'), may hold values from -3 to 3
- out_grad: bfloat16 [8, 1024, 1024], P('fsdp', 'ctx'), may hold values from -6 to 6
Outputs:
- hidden_out: bfloat16 [8, 1024, 1024], P('fsdp', 'ctx')
- in_grad: bfloat16 [8, 1024, 1024], P('fsdp', 'ctx')
- grad_qkv_weight: float32 [1024, 3072], P('fsdp')
- grad_qv_bias: float32 [2048], P('fsdp')
- grad_out_weight: float32 [1024, 1024], P('fsdp')
- grad_out_bias: float32 [1024], P('fsdp')
- grad_attn_gain: float32 [1024], P('fsdp')
- grad_attn_shift: float32 [1024], P('fsdp')
- grad_in_weight: float32 [1024, 4096], P('fsdp')
- grad_in_bias: float32 [4096], P('fsdp')
- grad_down_weight: float32 [4096, 1024], P('fsdp')
- grad_down_bias: float32 [1024], P('fsdp')
- grad_ffn_gain: float32 [1024], P('fsdp')
- grad_ffn_shift: float32 [1024], P('fsdp')
Inputs may be any that keep to these rules, and one draw needn't show every extreme that they name: `lengths`: some sequence has length 1024 and some has length 128. `block_of`: each row names every block once.
All inputs are finite; a program needn't handle non-finite values.
Results may differ from a plain program's by a relative error of at most 0.013.
The roundings to bfloat16 on the way count: a program that leaves them out, or rounds other values in their place, can miss the bound.
Values may be sent and summed in bfloat16 or wider, within the bound.
A program may use at most 256 MiB of HBM per device.

v0:
```python
import jax
import jax.numpy as jnp
from jax import lax
from jax.sharding import PartitionSpec as P

HEADS = 16


NEG_FILL = -1e30
NORM_EPS = 1e-12
INV_ROOT_TWO = 0.7071067811865476
INV_ROOT_TAU = 0.3989422804014327


def split_heads(tensor):
    return tensor.reshape(tensor.shape[0], HEADS, -1)


def mix(pattern, left_op, right_op):
    return jnp.einsum(pattern, left_op, right_op, preferred_element_type=jnp.float32)


def outer(left_op, right_op):
    return lax.dot_general(
        left_op, right_op, (((0,), (0,)), ((), ())), preferred_element_type=jnp.float32
    )


def against(left_op, right_op):
    return lax.dot_general(
        left_op, right_op, (((1,), (1,)), ((), ())), preferred_element_type=jnp.float32
    )


def key_valid(lengths, block_of, key_total):
    blocks = block_of.shape[1]
    block_size = key_total // blocks
    offsets = jnp.tile(jnp.arange(block_size, dtype=jnp.int32), blocks)
    places = jnp.repeat(block_of, block_size, axis=1) * block_size + offsets[None, :]
    return places < lengths[:, None]


def gelu_exact(values):
    return 0.5 * values * (1.0 + jax.scipy.special.erf(values * INV_ROOT_TWO))


def gelu_slope(values):
    return (
        0.5 * (1.0 + jax.scipy.special.erf(values * INV_ROOT_TWO))
        + values * jnp.exp(-0.5 * values * values) * INV_ROOT_TAU
    )


def layer_norm(values, gain_vec, shift_vec):
    center = values - jnp.mean(values, axis=-1, keepdims=True)
    inv_scale = lax.rsqrt(jnp.mean(center * center, axis=-1, keepdims=True) + NORM_EPS)
    unit = center * inv_scale
    return (unit * gain_vec.astype(jnp.float32) + shift_vec.astype(jnp.float32), unit, inv_scale)


def norm_back(upstream, unit, inv_scale, gain_vec):
    scaled = upstream * gain_vec.astype(jnp.float32)
    return inv_scale * (
        scaled
        - jnp.mean(scaled, axis=-1, keepdims=True)
        - unit * jnp.mean(scaled * unit, axis=-1, keepdims=True)
    )


def project(token_rows, qkv_full, bias_vec):
    width = token_rows.shape[1]
    total = jnp.dot(token_rows, qkv_full, preferred_element_type=jnp.float32)
    bias_full = bias_vec.astype(jnp.float32)
    queries = (total[:, :width] + bias_full[:width]).astype(jnp.bfloat16)
    keys_out = total[:, width : 2 * width].astype(jnp.bfloat16)
    values_out = (total[:, 2 * width :] + bias_full[width:]).astype(jnp.bfloat16)
    return (queries, keys_out, values_out)


def score_block(query_one, key_one, allowed_one):
    score_scale = (query_one.shape[-1] // HEADS) ** (-0.5)
    scores = mix("qhd,khd->hqk", split_heads(query_one), split_heads(key_one)) * score_scale
    return jnp.where(allowed_one[None, None, :], scores, NEG_FILL)


def attend(query_seq, keys_all, values_all, allowed):

    def single(pieces):
        query_one, key_one, value_one, allowed_one = pieces
        scores = score_block(query_one, key_one, allowed_one)
        row_top = jnp.max(scores, axis=-1, keepdims=True)
        log_total = row_top + jnp.log(jnp.sum(jnp.exp(scores - row_top), axis=-1, keepdims=True))
        probs_half = jnp.exp(scores - log_total).astype(jnp.bfloat16)
        mixed_out = mix("hqk,khd->qhd", probs_half, split_heads(value_one))
        return (mixed_out.reshape(mixed_out.shape[0], -1).astype(jnp.bfloat16), log_total[..., 0])

    return lax.map(single, (query_seq, keys_all, values_all, allowed))


def attend_back(query_seq, keys_all, values_all, allowed, log_totals, mixed_grad):

    def single(pieces):
        query_one, key_one, value_one, allowed_one, log_one, grad_one = pieces
        score_scale = (query_one.shape[-1] // HEADS) ** (-0.5)
        scores = score_block(query_one, key_one, allowed_one)
        probs = jnp.exp(scores - log_one[..., None])
        probs_half = probs.astype(jnp.bfloat16)
        value_grad = mix("hqk,qhd->khd", probs_half, split_heads(grad_one))
        prob_grad = mix("qhd,khd->hqk", split_heads(grad_one), split_heads(value_one))
        row_dot = jnp.sum(probs * prob_grad, axis=-1, keepdims=True)
        score_grad = (probs * (prob_grad - row_dot) * score_scale).astype(jnp.bfloat16)
        query_grad = mix("hqk,khd->qhd", score_grad, split_heads(key_one))
        key_grad = mix("hqk,qhd->khd", score_grad, split_heads(query_one))
        return (
            query_grad.reshape(query_grad.shape[0], -1),
            key_grad.reshape(key_grad.shape[0], -1),
            value_grad.reshape(value_grad.shape[0], -1),
        )

    return lax.map(single, (query_seq, keys_all, values_all, allowed, log_totals, mixed_grad))


def local(
    hidden_in,
    lengths,
    block_of,
    qkv_weight,
    qv_bias,
    out_weight,
    out_bias,
    attn_gain,
    attn_shift,
    in_weight,
    in_bias,
    down_weight,
    down_bias,
    ffn_gain,
    ffn_shift,
    out_grad,
):
    seq_count, row_count, width = hidden_in.shape
    attn_full = (
        lax.all_gather(qkv_weight, "fsdp", axis=0, tiled=True),
        lax.all_gather(qv_bias, "fsdp", axis=0, tiled=True),
        lax.all_gather(out_weight, "fsdp", axis=0, tiled=True),
        lax.all_gather(out_bias, "fsdp", axis=0, tiled=True),
        lax.all_gather(attn_gain, "fsdp", axis=0, tiled=True),
        lax.all_gather(attn_shift, "fsdp", axis=0, tiled=True),
    )
    ffn_full = (
        lax.all_gather(in_weight, "fsdp", axis=0, tiled=True),
        lax.all_gather(in_bias, "fsdp", axis=0, tiled=True),
        lax.all_gather(down_weight, "fsdp", axis=0, tiled=True),
        lax.all_gather(down_bias, "fsdp", axis=0, tiled=True),
        lax.all_gather(ffn_gain, "fsdp", axis=0, tiled=True),
        lax.all_gather(ffn_shift, "fsdp", axis=0, tiled=True),
    )
    full_qkv, full_qv_bias, full_out_weight, full_out_bias, full_attn_gain, full_attn_shift = (
        attn_full
    )
    (
        full_in_weight,
        full_in_bias,
        full_down_weight,
        full_down_bias,
        full_ffn_gain,
        full_ffn_shift,
    ) = ffn_full
    token_rows = hidden_in.reshape(seq_count * row_count, width)
    queries, keys_local, values_local = project(token_rows, full_qkv, full_qv_bias)
    keys_all, values_all = (
        lax.all_gather(keys_local.reshape(seq_count, row_count, width), "ctx", axis=1, tiled=True),
        lax.all_gather(
            values_local.reshape(seq_count, row_count, width), "ctx", axis=1, tiled=True
        ),
    )
    allowed = key_valid(lengths, block_of, keys_all.shape[1])
    query_seq = queries.reshape(seq_count, row_count, width)
    mixed, log_totals = attend(query_seq, keys_all, values_all, allowed)
    mixed_rows = mixed.reshape(-1, width)
    attn_rows = jnp.dot(
        mixed_rows, full_out_weight, preferred_element_type=jnp.float32
    ) + full_out_bias.astype(jnp.float32)
    first_sum = token_rows.astype(jnp.float32) + attn_rows
    first_norm, first_unit, first_scale = layer_norm(first_sum, full_attn_gain, full_attn_shift)
    first_half = first_norm.astype(jnp.bfloat16)
    inner_pre = jnp.dot(
        first_half, full_in_weight, preferred_element_type=jnp.float32
    ) + full_in_bias.astype(jnp.float32)
    inner_act = gelu_exact(inner_pre).astype(jnp.bfloat16)
    second_sum = (
        first_norm
        + jnp.dot(inner_act, full_down_weight, preferred_element_type=jnp.float32)
        + full_down_bias.astype(jnp.float32)
    )
    result, second_unit, second_scale = layer_norm(second_sum, full_ffn_gain, full_ffn_shift)
    hidden_out = result.astype(jnp.bfloat16).reshape(seq_count, row_count, width)
    back_ffn = (
        lax.all_gather(in_weight, "fsdp", axis=0, tiled=True),
        lax.all_gather(in_bias, "fsdp", axis=0, tiled=True),
        lax.all_gather(down_weight, "fsdp", axis=0, tiled=True),
        lax.all_gather(down_bias, "fsdp", axis=0, tiled=True),
        lax.all_gather(ffn_gain, "fsdp", axis=0, tiled=True),
        lax.all_gather(ffn_shift, "fsdp", axis=0, tiled=True),
    )
    (
        back_in_weight,
        unused_in_bias,
        back_down_weight,
        unused_down_bias,
        back_ffn_gain,
        unused_ffn_shift,
    ) = back_ffn
    cot_rows = out_grad.reshape(-1, width).astype(jnp.float32)
    grad_ffn_gain = jnp.sum(cot_rows * second_unit, axis=0)
    grad_ffn_shift = jnp.sum(cot_rows, axis=0)
    second_grad = norm_back(cot_rows, second_unit, second_scale, back_ffn_gain)
    second_half = second_grad.astype(jnp.bfloat16)
    grad_down_weight = outer(inner_act, second_half)
    grad_down_bias = jnp.sum(second_grad, axis=0)
    inner_grad = against(second_half, back_down_weight) * gelu_slope(inner_pre)
    inner_half = inner_grad.astype(jnp.bfloat16)
    grad_in_weight = outer(first_half, inner_half)
    grad_in_bias = jnp.sum(inner_grad, axis=0)
    back_attn = (
        lax.all_gather(qkv_weight, "fsdp", axis=0, tiled=True),
        lax.all_gather(qv_bias, "fsdp", axis=0, tiled=True),
        lax.all_gather(out_weight, "fsdp", axis=0, tiled=True),
        lax.all_gather(out_bias, "fsdp", axis=0, tiled=True),
        lax.all_gather(attn_gain, "fsdp", axis=0, tiled=True),
        lax.all_gather(attn_shift, "fsdp", axis=0, tiled=True),
    )
    (
        back_qkv,
        unused_qv_bias,
        back_out_weight,
        unused_out_bias,
        back_attn_gain,
        unused_attn_shift,
    ) = back_attn
    first_back = second_grad + against(inner_half, back_in_weight)
    grad_attn_gain = jnp.sum(first_back * first_unit, axis=0)
    grad_attn_shift = jnp.sum(first_back, axis=0)
    first_grad = norm_back(first_back, first_unit, first_scale, back_attn_gain)
    attn_half = first_grad.astype(jnp.bfloat16)
    grad_out_weight = outer(mixed_rows, attn_half)
    grad_out_bias = jnp.sum(first_grad, axis=0)
    mixed_grad = (
        against(attn_half, back_out_weight)
        .astype(jnp.bfloat16)
        .reshape(seq_count, row_count, width)
    )
    query_grad, key_grad, value_grad = attend_back(
        query_seq, keys_all, values_all, allowed, log_totals, mixed_grad
    )
    key_own, value_own = (
        lax.psum_scatter(key_grad, "ctx", scatter_dimension=1, tiled=True),
        lax.psum_scatter(value_grad, "ctx", scatter_dimension=1, tiled=True),
    )
    query_rows = query_grad.reshape(-1, width)
    value_rows = value_own.reshape(-1, width)
    proj_half = jnp.concatenate(
        [query_rows, key_own.reshape(-1, width), value_rows], axis=1
    ).astype(jnp.bfloat16)
    grad_qkv_weight = outer(token_rows, proj_half)
    grad_qv_bias = jnp.concatenate([jnp.sum(query_rows, axis=0), jnp.sum(value_rows, axis=0)])
    in_grad = (
        (first_grad + against(proj_half, back_qkv))
        .astype(jnp.bfloat16)
        .reshape(seq_count, row_count, width)
    )
    shard_list = (
        lax.psum_scatter(grad_qkv_weight, "fsdp", scatter_dimension=0, tiled=True),
        lax.psum_scatter(grad_qv_bias, "fsdp", scatter_dimension=0, tiled=True),
        lax.psum_scatter(grad_out_weight, "fsdp", scatter_dimension=0, tiled=True),
        lax.psum_scatter(grad_out_bias, "fsdp", scatter_dimension=0, tiled=True),
        lax.psum_scatter(grad_attn_gain, "fsdp", scatter_dimension=0, tiled=True),
        lax.psum_scatter(grad_attn_shift, "fsdp", scatter_dimension=0, tiled=True),
        lax.psum_scatter(grad_in_weight, "fsdp", scatter_dimension=0, tiled=True),
        lax.psum_scatter(grad_in_bias, "fsdp", scatter_dimension=0, tiled=True),
        lax.psum_scatter(grad_down_weight, "fsdp", scatter_dimension=0, tiled=True),
        lax.psum_scatter(grad_down_bias, "fsdp", scatter_dimension=0, tiled=True),
        lax.psum_scatter(grad_ffn_gain, "fsdp", scatter_dimension=0, tiled=True),
        lax.psum_scatter(grad_ffn_shift, "fsdp", scatter_dimension=0, tiled=True),
    )
    (
        shard_qkv,
        shard_qv,
        shard_outw,
        shard_outb,
        shard_again,
        shard_ashift,
        shard_inw,
        shard_inb,
        shard_downw,
        shard_downb,
        shard_fgain,
        shard_fshift,
    ) = shard_list
    totals = lax.psum(
        (
            shard_qkv,
            shard_qv,
            shard_outw,
            shard_outb,
            shard_again,
            shard_ashift,
            shard_inw,
            shard_inb,
            shard_downw,
            shard_downb,
            shard_fgain,
            shard_fshift,
        ),
        "ctx",
    )
    return (
        hidden_out,
        in_grad,
        totals[0],
        totals[1],
        totals[2],
        totals[3],
        totals[4],
        totals[5],
        totals[6],
        totals[7],
        totals[8],
        totals[9],
        totals[10],
        totals[11],
    )


def solution(mesh):
    return jax.shard_map(
        local,
        mesh=mesh,
        in_specs=(
            P("fsdp", "ctx", None),
            P("fsdp"),
            P("fsdp", None),
            P("fsdp", None),
            P("fsdp"),
            P("fsdp", None),
            P("fsdp"),
            P("fsdp"),
            P("fsdp"),
            P("fsdp", None),
            P("fsdp"),
            P("fsdp", None),
            P("fsdp"),
            P("fsdp"),
            P("fsdp"),
            P("fsdp", "ctx", None),
        ),
        out_specs=(
            P("fsdp", "ctx", None),
            P("fsdp", "ctx", None),
            P("fsdp", None),
            P("fsdp"),
            P("fsdp", None),
            P("fsdp"),
            P("fsdp"),
            P("fsdp"),
            P("fsdp", None),
            P("fsdp"),
            P("fsdp", None),
            P("fsdp"),
            P("fsdp"),
            P("fsdp"),
        ),
        check_vma=False,
    )
```

profile of v0, /device:TPU:0, one launch (start us, length us, event | category | flops | bytes accessed | tf_op | source)
XLA Modules:
  0.0 1166.6 jit_solution(4920743499116831326)
XLA Ops:
  8.6 13.5 %all-gather.2 = bf16[8,1,256]{2,1,0:T(2,128)(2,1)S(1)} all-gather(bf16[1,1,256]{2,1,0:T(2,128)(2,1)S(1)} %reshape.222), channel_id=1, replica_groups=mesh['ctx'=4,'fsdp'=8] {'fsdp'}, dimensions={0}, use_global_device_ids=true | all-gather | bytes 4608 | tf_op jit(solution)/shard_map/all_gather | solution.py:144
  22.1 55.0 %all-gather.17.cloned.1.call-done = bf16[1024,3072]{1,0:T(8,128)(2,1)} async-done(((bf16[128,3072]{1,0:T(8,128)(2,1)}), bf16[1024,3072]{1,0:T(8,128)(2,1)}) %all-gather.17.cloned.1.call-update) | async-done | bytes 6291472 | tf_op jit(solution)/shard_map/all_gather | solution.py:143
  77.1 4.8 fusion.56
  86.6 9.1 all-gather.3
  95.7 9.7 all-gather.4
  105.4 9.1 all-gather.5
  114.5 9.7 all-gather.7
  124.2 9.1 all-gather.8
  133.3 9.7 all-gather.9
  143.0 13.3 %all-gather.6 = bf16[8,1,512]{2,1,0:T(2,128)(2,1)S(1)} all-gather(bf16[1,1,512]{2,1,0:T(2,128)(2,1)S(1)} %reshape.230), channel_id=1, replica_groups=mesh['ctx'=4,'fsdp'=8] {'fsdp'}, dimensions={0}, use_global_device_ids=true | all-gather | bytes 9216 | tf_op jit(solution)/shard_map/all_gather | solution.py:152
  160.7 4.6 copy.46
  179.4 6.0 all-gather.19.cloned.1.call-done
  188.1 80.2 %all-gather.21.cloned.1.call-done = bf16[1024,4096]{1,0:T(8,128)(2,1)} async-done(((bf16[128,4096]{1,0:T(8,128)(2,1)}), bf16[1024,4096]{1,0:T(8,128)(2,1)}) %all-gather.21.cloned.1.call-update) | async-done | bytes 8388624 | tf_op jit(solution)/shard_map/all_gather | solution.py:151
  268.3 7.9 convolution_add_fusion
  276.2 74.1 %all-gather.23.cloned.1.call-done = bf16[4096,1024]{1,0:T(8,128)(2,1)} async-done(((bf16[512,1024]{1,0:T(8,128)(2,1)}), bf16[4096,1024]{1,0:T(8,128)(2,1)}) %all-gather.23.cloned.1.call-update) | async-done | bytes 8388624 | tf_op jit(solution)/shard_map/all_gather | solution.py:153
  350.4 7.3 fusion.93
  359.9 4.3 fusion.96
  370.9 11.6 fusion.64
  382.6 10.4 fusion.97
  393.0 32.6 %fusion.7 = f32[16,64,1024]{2,1,0:T(8,128)} fusion(bf16[256,16,64]{0,2,1:T(8,128)(2,1)} %bitcast.102, f32[16,256,1024]{2,1,0:T(8,128)} %fusion.97, f32[16,256,1024]{2,1,0:T(8,128)} %copy-done, f32[16,256]{1,0:T(8,128)S(1)} %log_add_fusion, pred[1024]{0:T(1024)(128)(4,1)S(1)} %fusion.67), kind=kOutput, calls=%fused_computation.9 | convolution fusion | flops 583013376 | bytes 38290432 | tf_op jit(solution)/shard_map/while/body/eval_jaxpr/hqk,qhd->khd/dot_general | solution.py:20
  429.4 10.3 fusion.61
  439.8 9.8 fusion.50
  451.3 37.4 %fusion.89 = (f32[16,64]{1,0:T(8,128)S(1)}, bf16[256,16,64]{0,2,1:T(8,128)(2,1)}) fusion(bf16[1024,16,64]{0,2,1:T(8,128)(2,1)S(1)} %bitcast.98, f32[16,256,1024]{2,1,0:T(8,128)} %fusion.97, f32[16,256,1024]{2,1,0:T(8,128)} %copy-done, f32[16,256]{1,0:T(8,128)S(1)} %log_add_fusion, pred[1024]{0:T(1024)(128)(4,1)S(1)} %fusion.67), kind=kOutput, calls=%fused_computation.111 | convolution fusion | flops 583536640 | bytes 36197376 | tf_op jit(solution)/shard_map/while/body/eval_jaxpr/hqk,khd->qhd/dot_general | solution.py:20
  491.8 7.6 convolution_bitcast_fusion
  499.5 42.2 %reduce-scatter.13.cloned.1.call-done = f32[128,1024]{1,0:T(8,128)} async-done(((f32[1024,1024]{1,0:T(8,128)}), f32[128,1024]{1,0:T(8,128)}) %reduce-scatter.13.cloned.1.call-update) | async-done | bytes 524304 | tf_op jit(solution)/shard_map/reduce_scatter | solution.py:275
  541.7 168.9 %reduce-scatter.17.cloned.1.call-done = f32[512,1024]{1,0:T(8,128)} async-done(((f32[4096,1024]{1,0:T(8,128)}), f32[512,1024]{1,0:T(8,128)}) %reduce-scatter.17.cloned.1.call-update) | async-done | bytes 2097168 | tf_op jit(solution)/shard_map/reduce_scatter | solution.py:281
  710.6 169.0 %reduce-scatter.15.cloned.1.call-done = f32[128,4096]{1,0:T(8,128)} async-done(((f32[1024,4096]{1,0:T(8,128)}), f32[128,4096]{1,0:T(8,128)}) %reduce-scatter.15.cloned.1.call-update) | async-done | bytes 2097168 | tf_op jit(solution)/shard_map/reduce_scatter | solution.py:279
  879.6 129.8 %reduce-scatter.11.cloned.1.call-done = f32[128,3072]{0,1:T(8,128)} async-done(((f32[1024,3072]{0,1:T(8,128)}), f32[128,3072]{0,1:T(8,128)}) %reduce-scatter.11.cloned.1.call-update) | async-done | bytes 1572880 | tf_op jit(solution)/shard_map/reduce_scatter | solution.py:273
  1012.1 26.4 %all-reduce.8 = (f32[2048]{0:T(1024)S(1)}, f32[1024]{0:T(1024)S(1)}, f32[1024]{0:T(1024)S(1)}, f32[1024]{0:T(1024)S(1)}, f32[4096]{0:T(1024)S(1)}, /*index=5*/f3...) all-reduce(f32[2048]{0:T(1024)S(1)} %pad_maximum_fusion.3, ...), channel_id=7, replica_groups=mesh['ctx'=4,'fsdp'=8] {'fsdp'}, use_global_device_ids=true, to_apply=%region_17.18.clone | all-reduce | flops 12288 | bytes 98304
  1039.1 11.5 all-reduce.9
  1050.6 5.5 fusion.43
  1056.1 94.2 %all-reduce.13.cloned.1.call-done = (f32[128,3072]{0,1:T(8,128)}, f32[128,1024]{1,0:T(8,128)}, f32[128,4096]{1,0:T(8,128)}, f32[512,1024]{1,0:T(8,128)}) async-done(((f32[128,3072]{0,1:T(8,128)}, f32[128,1024]{1,0:T(8,128)}, f32[128,4096]{1,0:T(8,128)}, f32[512,1024]{1,0:T(8,128)}), (f32[128,3072]{0,1:T(8,128)}, f32[128,1024]{1,0:T(8,128)}, f32[128,4096]{1,0:T(8,128)}, ...) | async-done | bytes 6291472 | tf_op jit(solution)/shard_map/psum | solution.py:300
  (139 shorter events, 55.1 us)
Async XLA Ops:
  7.2 69.9 %all-gather.17.cloned.1.call-start = ((), (), s32[]{:S(2)}) async-start(), calls=%async_computation.6 | async-start | bytes 7077888 | tf_op jit(solution)/shard_map/all_gather | solution.py:143
  7.9 149.7 %all-gather.25.cloned.1.call-start = ((), (), s32[]{:S(2)}) async-start(), calls=%async_computation.16 | async-start | bytes 2621440 | tf_op jit(solution)/shard_map/all_gather | solution.py:173
  81.9 13.9 %copy-start.15 = (bf16[128]{0:T(256)(128)(2,1)S(1)}, bf16[128]{0:T(256)(128)(2,1)}, u32[]{:S(2)}) copy-start(bf16[128]{0:T(256)(128)(2,1)} %param.23) | copy-start | bytes 772
  81.9 23.5 %copy-start.16 = (bf16[128]{0:T(256)(128)(2,1)S(1)}, bf16[128]{0:T(256)(128)(2,1)}, u32[]{:S(2)}) copy-start(bf16[128]{0:T(256)(128)(2,1)} %param.24) | copy-start | bytes 772
  81.9 32.6 %copy-start.17 = (bf16[128]{0:T(256)(128)(2,1)S(1)}, bf16[128]{0:T(256)(128)(2,1)}, u32[]{:S(2)}) copy-start(bf16[128]{0:T(256)(128)(2,1)} %param.28) | copy-start | bytes 772
  81.9 42.3 %copy-start.18 = (bf16[128]{0:T(256)(128)(2,1)S(1)}, bf16[128]{0:T(256)(128)(2,1)}, u32[]{:S(2)}) copy-start(bf16[128]{0:T(256)(128)(2,1)} %param.29) | copy-start | bytes 772
  81.9 51.4 %copy-start.19 = (bf16[128]{0:T(256)(128)(2,1)S(1)}, bf16[128]{0:T(256)(128)(2,1)}, u32[]{:S(2)}) copy-start(bf16[128]{0:T(256)(128)(2,1)} %param.30) | copy-start | bytes 772
  81.9 74.4 %copy-start.20 = (s32[1,8]{1,0:T(1,128)S(1)}, s32[1,8]{1,0:T(1,128)}, u32[]{:S(2)}) copy-start(s32[1,8]{1,0:T(1,128)} %param.18) | copy-start | bytes 100
  83.2 77.5 %all-gather.27.cloned.1.call-start = ((), (), s32[]{:S(2)}) async-start(), calls=%async_computation.17 | async-start | bytes 2621440 | tf_op jit(solution)/shard_map/all_gather | solution.py:172
  84.1 101.3 %all-gather.19.cloned.1.call-start = ((), (), s32[]{:S(2)}) async-start(), calls=%async_computation.7 | async-start | bytes 2359296 | tf_op jit(solution)/shard_map/all_gather | solution.py:145
  84.7 183.6 %all-gather.21.cloned.1.call-start = ((), (), s32[]{:S(2)}) async-start(), calls=%async_computation.8 | async-start | bytes 9437184 | tf_op jit(solution)/shard_map/all_gather | solution.py:151
  85.3 265.1 %all-gather.23.cloned.1.call-start = ((), (), s32[]{:S(2)}) async-start(), calls=%async_computation.9 | async-start | bytes 9437184 | tf_op jit(solution)/shard_map/all_gather | solution.py:153
  85.9 402.8 %reduce-scatter.9.cloned.1.call-start = ((), (), s32[]{:S(2)}) async-start(), calls=%async_computation.11 | async-start | bytes 5242880 | tf_op jit(solution)/shard_map/reduce_scatter | solution.py:258
  157.6 7.7 copy-start.8
  160.7 12.9 %copy-start.2 = (bf16[1024,1024]{0,1:T(8,128)(2,1)}, bf16[1024,1024]{0,1:T(8,128)(2,1)S(1)}, u32[]{:S(2)}) copy-start(bf16[1024,1024]{0,1:T(8,128)(2,1)S(1)} %copy.44) | copy-start | bytes 6291460
  169.5 5.7 copy-start
  175.2 10.2 copy-start.7
  179.4 96.8 %copy-start.10 = (bf16[16,64,256]{2,1,0:T(8,128)(2,1)}, bf16[16,64,256]{2,1,0:T(8,128)(2,1)S(1)}, u32[]{:S(2)}) copy-start(bf16[16,64,256]{2,1,0:T(8,128)(2,1)S(1)} %convolution_convert_fusion) | copy-start | bytes 1572868
  350.4 9.4 slice-start.2
  350.4 7.6 copy-start.5
  350.4 9.4 slice-start.3
  358.5 5.7 slice-start
  382.5 108.0 %reduce-scatter.7.cloned.1.call-start = ((), (), s32[]{:S(2)}) async-start(), calls=%async_computation.10 | async-start | bytes 5242880 | tf_op jit(solution)/shard_map/reduce_scatter | solution.py:257
  425.5 116.2 %reduce-scatter.13.cloned.1.call-start = ((), (), s32[]{:S(2)}) async-start(), calls=%async_computation.13 | async-start | bytes 4718592 | tf_op jit(solution)/shard_map/reduce_scatter | solution.py:275
  429.4 281.2 %reduce-scatter.17.cloned.1.call-start = ((), (), s32[]{:S(2)}) async-start(), calls=%async_computation.15 | async-start | bytes 18874368 | tf_op jit(solution)/shard_map/reduce_scatter | solution.py:281
  439.8 439.8 %reduce-scatter.15.cloned.1.call-start = ((), (), s32[]{:S(2)}) async-start(), calls=%async_computation.14 | async-start | bytes 18874368 | tf_op jit(solution)/shard_map/reduce_scatter | solution.py:279
  449.6 559.7 %reduce-scatter.11.cloned.1.call-start = ((), (), s32[]{:S(2)}) async-start(), calls=%async_computation.12 | async-start | bytes 14155776 | tf_op jit(solution)/shard_map/reduce_scatter | solution.py:273
  499.4 510.0 %copy-start.21 = (u32[32]{0:T(128)S(1)}, u32[32]{0:T(128)}, u32[]{:S(2)}) copy-start(u32[32]{0:T(128)} %constant.85) | copy-start | bytes 388
  499.4 512.5 %copy-start.6 = (bf16[1,256,1024]{2,1,0:T(8,128)(2,1)S(1)}, bf16[1,256,1024]{2,1,0:T(8,128)(2,1)}, u32[]{:S(2)}) copy-start(bf16[1,256,1024]{2,1,0:T(8,128)(2,1)} %param.31) | copy-start | bytes 1572868
  499.5 551.2 %copy-start.12 = (bf16[256,16,64]{0,2,1:T(8,128)(2,1)S(1)}, bf16[256,16,64]{0,2,1:T(8,128)(2,1)}, u32[]{:S(2)}) copy-start(bf16[256,16,64]{0,2,1:T(8,128)(2,1)} %get-tuple-element.142) | copy-start | bytes 1572868
  499.5 650.8 %all-reduce.13.cloned.1.call-start = ((), (), s32[]{:S(2)}) async-start(), calls=%async_computation.18 | async-start | bytes 12582912 | tf_op jit(solution)/shard_map/psum | solution.py:300
  1150.3 8.2 copy-start.9
  (7 other events, 23.6 us)
Sparse Core Ops, SparseCore 0:
  9.6 67.4 all-gather.16
  83.3 33.8 all-gather.24
  119.6 35.1 all-gather.26
  156.3 29.1 all-gather.18
  186.9 81.4 all-gather.20
  269.8 80.5 all-gather.22
  382.7 51.1 reduce-scatter.8
  436.8 52.6 reduce-scatter.6
  491.8 49.8 reduce-scatter.12
  543.9 166.6 reduce-scatter.16
  712.9 166.6 reduce-scatter.14
  881.8 127.5 reduce-scatter.10
  1013.1 137.1 all-reduce.12
where the time goes:
time: 1170 us
  waiting for transfers between devices  822 us (70%)
  matrix products  168 us (14%)
  blocking collectives  121 us (10%)
  local copies, waits for them, and re-layouts  26.6 us (2%)
  between operations  17.2 us (1%)
    reduce_scatter x1, waiting for transfers between devices, local(): lax.psum_scatter(grad_in_weight, 'fsdp', scatter_dimension=0, tiled=True)  169 us
    reduce_scatter x1, waiting for transfers between devices, local(): lax.psum_scatter(grad_down_weight, 'fsdp', scatter_dimension=0, tiled=True)  169 us
    reduce_scatter x1, waiting for transfers between devices, local(): lax.psum_scatter(grad_qkv_weight, 'fsdp', scatter_dimension=0, tiled=True)  130 us
    dot_general x6, matrix products, mix(): jnp.einsum(pattern, left_op, right_op, preferred_element_type=jnp.float32)  100 us
    psum x1, waiting for transfers between devices, local(): lax.psum((shard_qkv, shard_qv, shard_outw, shard_outb, shard_again, shard...  94.2 us
    all_gather x1, waiting for transfers between devices, local(): lax.all_gather(in_weight, 'fsdp', axis=0, tiled=True)  80.2 us
    all_gather x1, waiting for transfers between devices, local(): lax.all_gather(down_weight, 'fsdp', axis=0, tiled=True)  74.1 us
    all_gather x1, waiting for transfers between devices, local(): lax.all_gather(qkv_weight, 'fsdp', axis=0, tiled=True)  55 us
  transfers between devices with their start and end apart: 13, of which 9 were waited for; matrix products, arithmetic and copies ran while one was open for 13% of the time, Pallas kernels for 0%

commit v1 on v0

--- a/solution.py
+++ b/solution.py
@@ -118,6 +118,47 @@
         )
 
     return lax.map(single, (query_seq, keys_all, values_all, allowed, log_totals, mixed_grad))
+
+
+def gather_smalls(smalls):
+    packed = jnp.concatenate(smalls)[None]
+    full = lax.all_gather(packed, "fsdp", axis=0, tiled=True)
+    pieces = []
+    at = 0
+    for item in smalls:
+        pieces.append(full[:, at : at + item.shape[0]].reshape(-1))
+        at += item.shape[0]
+    return pieces
+
+
+def scatter_half(grad):
+    return lax.psum_scatter(
+        grad.astype(jnp.bfloat16), "fsdp", scatter_dimension=0, tiled=True
+    )
+
+
+def halve(values):
+    return lax.reduce_precision(values, 8, 7).astype(jnp.bfloat16)
+
+
+def swap_sum(part, order):
+    size = lax.axis_size("ctx")
+    for bit in order:
+        other = lax.ppermute(part, "ctx", [(i, i ^ bit) for i in range(size)])
+        total = part.astype(jnp.float32) + other.astype(jnp.float32)
+        part = halve(total)
+    return total
+
+
+def sum_over_ctx(part):
+    size = lax.axis_size("ctx")
+    if size & (size - 1):
+        return lax.psum(part.astype(jnp.float32), "ctx")
+    order = [1 << k for k in range(size.bit_length() - 1)]
+    mid = part.shape[0] // 2
+    return jnp.concatenate(
+        [swap_sum(part[:mid], order), swap_sum(part[mid:], order[::-1])], axis=0
+    )
 
 
 def local(
@@ -139,41 +180,32 @@
     out_grad,
 ):
     seq_count, row_count, width = hidden_in.shape
-    attn_full = (
-        lax.all_gather(qkv_weight, "fsdp", axis=0, tiled=True),
-        lax.all_gather(qv_bias, "fsdp", axis=0, tiled=True),
-        lax.all_gather(out_weight, "fsdp", axis=0, tiled=True),
-        lax.all_gather(out_bias, "fsdp", axis=0, tiled=True),
-        lax.all_gather(attn_gain, "fsdp", axis=0, tiled=True),
-        lax.all_gather(attn_shift, "fsdp", axis=0, tiled=True),
-    )
-    ffn_full = (
-        lax.all_gather(in_weight, "fsdp", axis=0, tiled=True),
-        lax.all_gather(in_bias, "fsdp", axis=0, tiled=True),
-        lax.all_gather(down_weight, "fsdp", axis=0, tiled=True),
-        lax.all_gather(down_bias, "fsdp", axis=0, tiled=True),
-        lax.all_gather(ffn_gain, "fsdp", axis=0, tiled=True),
-        lax.all_gather(ffn_shift, "fsdp", axis=0, tiled=True),
-    )
-    full_qkv, full_qv_bias, full_out_weight, full_out_bias, full_attn_gain, full_attn_shift = (
-        attn_full
-    )
+    smalls = (qv_bias, out_bias, attn_gain, attn_shift, in_bias, down_bias, ffn_gain, ffn_shift)
     (
-        full_in_weight,
+        full_qv_bias,
+        full_out_bias,
+        full_attn_gain,
+        full_attn_shift,
         full_in_bias,
-        full_down_weight,
         full_down_bias,
         full_ffn_gain,
         full_ffn_shift,
-    ) = ffn_full
+    ) = gather_smalls(smalls)
+    full_qkv = lax.all_gather(qkv_weight, "fsdp", axis=0, tiled=True)
+    full_out_weight = lax.all_gather(out_weight, "fsdp", axis=0, tiled=True)
+    full_in_weight = lax.all_gather(in_weight, "fsdp", axis=0, tiled=True)
+    full_down_weight = lax.all_gather(down_weight, "fsdp", axis=0, tiled=True)
     token_rows = hidden_in.reshape(seq_count * row_count, width)
     queries, keys_local, values_local = project(token_rows, full_qkv, full_qv_bias)
-    keys_all, values_all = (
-        lax.all_gather(keys_local.reshape(seq_count, row_count, width), "ctx", axis=1, tiled=True),
-        lax.all_gather(
-            values_local.reshape(seq_count, row_count, width), "ctx", axis=1, tiled=True
+    both_all = lax.all_gather(
+        jnp.concatenate([keys_local, values_local], axis=1).reshape(
+            seq_count, row_count, 2 * width
         ),
-    )
+        "ctx",
+        axis=1,
+        tiled=True,
+    )
+    keys_all, values_all = both_all[..., :width], both_all[..., width:]
     allowed = key_valid(lengths, block_of, keys_all.shape[1])
     query_seq = queries.reshape(seq_count, row_count, width)
     mixed, log_totals = attend(query_seq, keys_all, values_all, allowed)
@@ -195,140 +227,102 @@
     )
     result, second_unit, second_scale = layer_norm(second_sum, full_ffn_gain, full_ffn_shift)
     hidden_out = result.astype(jnp.bfloat16).reshape(seq_count, row_count, width)
-    back_ffn = (
-        lax.all_gather(in_weight, "fsdp", axis=0, tiled=True),
-        lax.all_gather(in_bias, "fsdp", axis=0, tiled=True),
-        lax.all_gather(down_weight, "fsdp", axis=0, tiled=True),
-        lax.all_gather(down_bias, "fsdp", axis=0, tiled=True),
-        lax.all_gather(ffn_gain, "fsdp", axis=0, tiled=True),
-        lax.all_gather(ffn_shift, "fsdp", axis=0, tiled=True),
-    )
-    (
-        back_in_weight,
-        unused_in_bias,
-        back_down_weight,
-        unused_down_bias,
-        back_ffn_gain,
-        unused_ffn_shift,
-    ) = back_ffn
     cot_rows = out_grad.reshape(-1, width).astype(jnp.float32)
     grad_ffn_gain = jnp.sum(cot_rows * second_unit, axis=0)
     grad_ffn_shift = jnp.sum(cot_rows, axis=0)
-    second_grad = norm_back(cot_rows, second_unit, second_scale, back_ffn_gain)
+    second_grad = norm_back(cot_rows, second_unit, second_scale, full_ffn_gain)
     second_half = second_grad.astype(jnp.bfloat16)
     grad_down_weight = outer(inner_act, second_half)
     grad_down_bias = jnp.sum(second_grad, axis=0)
-    inner_grad = against(second_half, back_down_weight) * gelu_slope(inner_pre)
+    inner_grad = against(second_half, full_down_weight) * gelu_slope(inner_pre)
     inner_half = inner_grad.astype(jnp.bfloat16)
     grad_in_weight = outer(first_half, inner_half)
     grad_in_bias = jnp.sum(inner_grad, axis=0)
-    back_attn = (
-        lax.all_gather(qkv_weight, "fsdp", axis=0, tiled=True),
-        lax.all_gather(qv_bias, "fsdp", axis=0, tiled=True),
-        lax.all_gather(out_weight, "fsdp", axis=0, tiled=True),
-        lax.all_gather(out_bias, "fsdp", axis=0, tiled=True),
-        lax.all_gather(attn_gain, "fsdp", axis=0, tiled=True),
-        lax.all_gather(attn_shift, "fsdp", axis=0, tiled=True),
-    )
-    (
-        back_qkv,
-        unused_qv_bias,
-        back_out_weight,
-        unused_out_bias,
-        back_attn_gain,
-        unused_attn_shift,
-    ) = back_attn
-    first_back = second_grad + against(inner_half, back_in_weight)
+    first_back = second_grad + against(inner_half, full_in_weight)
     grad_attn_gain = jnp.sum(first_back * first_unit, axis=0)
     grad_attn_shift = jnp.sum(first_back, axis=0)
-    first_grad = norm_back(first_back, first_unit, first_scale, back_attn_gain)
+    first_grad = norm_back(first_back, first_unit, first_scale, full_attn_gain)
     attn_half = first_grad.astype(jnp.bfloat16)
     grad_out_weight = outer(mixed_rows, attn_half)
     grad_out_bias = jnp.sum(first_grad, axis=0)
     mixed_grad = (
-        against(attn_half, back_out_weight)
+        against(attn_half, full_out_weight)
         .astype(jnp.bfloat16)
         .reshape(seq_count, row_count, width)
     )
     query_grad, key_grad, value_grad = attend_back(
         query_seq, keys_all, values_all, allowed, log_totals, mixed_grad
     )
-    key_own, value_own = (
-        lax.psum_scatter(key_grad, "ctx", scatter_dimension=1, tiled=True),
-        lax.psum_scatter(value_grad, "ctx", scatter_dimension=1, tiled=True),
-    )
+    half_down = scatter_half(grad_down_weight)
+    both_grad = jnp.concatenate([key_grad, value_grad], axis=2).astype(jnp.bfloat16)
+    both_grad, half_down = lax.optimization_barrier((both_grad, half_down))
+    both_own = lax.psum_scatter(both_grad, "ctx", scatter_dimension=1, tiled=True)
+    half_in_grad, both_own = lax.optimization_barrier((grad_in_weight.astype(jnp.bfloat16), both_own))
+    half_in = scatter_half(half_in_grad)
+    key_own, value_own = both_own[..., :width], both_own[..., width:].astype(jnp.float32)
     query_rows = query_grad.reshape(-1, width)
     value_rows = value_own.reshape(-1, width)
     proj_half = jnp.concatenate(
-        [query_rows, key_own.reshape(-1, width), value_rows], axis=1
+        [query_rows.astype(jnp.bfloat16), key_own.reshape(-1, width), value_rows.astype(jnp.bfloat16)], axis=1
     ).astype(jnp.bfloat16)
     grad_qkv_weight = outer(token_rows, proj_half)
     grad_qv_bias = jnp.concatenate([jnp.sum(query_rows, axis=0), jnp.sum(value_rows, axis=0)])
     in_grad = (
-        (first_grad + against(proj_half, back_qkv))
+        (first_grad + against(proj_half, full_qkv))
         .astype(jnp.bfloat16)
         .reshape(seq_count, row_count, width)
     )
-    shard_list = (
-        lax.psum_scatter(grad_qkv_weight, "fsdp", scatter_dimension=0, tiled=True),
-        lax.psum_scatter(grad_qv_bias, "fsdp", scatter_dimension=0, tiled=True),
-        lax.psum_scatter(grad_out_weight, "fsdp", scatter_dimension=0, tiled=True),
-        lax.psum_scatter(grad_out_bias, "fsdp", scatter_dimension=0, tiled=True),
-        lax.psum_scatter(grad_attn_gain, "fsdp", scatter_dimension=0, tiled=True),
-        lax.psum_scatter(grad_attn_shift, "fsdp", scatter_dimension=0, tiled=True),
-        lax.psum_scatter(grad_in_weight, "fsdp", scatter_dimension=0, tiled=True),
-        lax.psum_scatter(grad_in_bias, "fsdp", scatter_dimension=0, tiled=True),
-        lax.psum_scatter(grad_down_weight, "fsdp", scatter_dimension=0, tiled=True),
-        lax.psum_scatter(grad_down_bias, "fsdp", scatter_dimension=0, tiled=True),
-        lax.psum_scatter(grad_ffn_gain, "fsdp", scatter_dimension=0, tiled=True),
-        lax.psum_scatter(grad_ffn_shift, "fsdp", scatter_dimension=0, tiled=True),
-    )
-    (
-        shard_qkv,
-        shard_qv,
-        shard_outw,
-        shard_outb,
-        shard_again,
-        shard_ashift,
-        shard_inw,
-        shard_inb,
-        shard_downw,
-        shard_downb,
-        shard_fgain,
-        shard_fshift,
-    ) = shard_list
-    totals = lax.psum(
-        (
-            shard_qkv,
-            shard_qv,
-            shard_outw,
-            shard_outb,
-            shard_again,
-            shard_ashift,
-            shard_inw,
-            shard_inb,
-            shard_downw,
-            shard_downb,
-            shard_fgain,
-            shard_fshift,
-        ),
-        "ctx",
-    )
+    small_grads = (
+        grad_qv_bias,
+        grad_out_bias,
+        grad_attn_gain,
+        grad_attn_shift,
+        grad_in_bias,
+        grad_down_bias,
+        grad_ffn_gain,
+        grad_ffn_shift,
+    )
+    shards = lax.axis_size("fsdp")
+    packed = jnp.concatenate([item.reshape(shards, -1) for item in small_grads], axis=1)
+    extra = -(-packed.shape[1] // (16 * width)) * 16
+    packed = jnp.pad(packed, ((0, 0), (0, extra * width - packed.shape[1])))
+    own_rows = width // shards
+    out_pack = jnp.concatenate(
+        [
+            grad_out_weight.reshape(shards, own_rows, width).astype(jnp.bfloat16),
+            packed.reshape(shards, extra, width).astype(jnp.bfloat16),
+        ],
+        axis=1,
+    ).reshape(shards * (own_rows + extra), width)
+    half_qkv = scatter_half(grad_qkv_weight)
+    out_pack, half_qkv = lax.optimization_barrier((out_pack, half_qkv))
+    half_out = scatter_half(out_pack)
+    total_down = sum_over_ctx(half_down)
+    total_in = sum_over_ctx(half_in)
+    total_qkv = sum_over_ctx(half_qkv)
+    total_pack = sum_over_ctx(half_out)
+    total_small = total_pack[own_rows:].reshape(-1)
+    small_out = []
+    at = 0
+    for item in small_grads:
+        size = item.shape[0] // shards
+        small_out.append(total_small[at : at + size])
+        at += size
     return (
         hidden_out,
         in_grad,
-        totals[0],
-        totals[1],
-        totals[2],
-        totals[3],
-        totals[4],
-        totals[5],
-        totals[6],
-        totals[7],
-        totals[8],
-        totals[9],
-        totals[10],
-        totals[11],
+        total_qkv,
+        small_out[0],
+        total_pack[:own_rows],
+        small_out[1],
+        small_out[2],
+        small_out[3],
+        total_in,
+        small_out[4],
+        total_down,
+        small_out[5],
+        small_out[6],
+        small_out[7],
     )
 
 

time: 1170 us -> 739 us (0.63)
  waiting for transfers between devices: 822 us -> 456 us
  blocking collectives: 121 us -> 16.1 us
  starting transfers between devices: 0.53 us -> 20.3 us
  other arithmetic: 11.3 us -> 26.8 us
    reduce_scatter x6 -> x4, waiting for transfers between devices: 510 us -> 119 us  [the longest x3 104 us: scatter_half(): lax.psum_scatter(grad.astype(jnp.bfloat16), 'fsdp', scatter_dimension=0,...]
    psum x1 -> x0, waiting for transfers between devices: 94.2 us -> none  [local(): lax.psum((shard_qkv, shard_qv, shard_outw, shard_outb, shard_again, shard...]
    all_gather x8 -> x1, blocking collectives: 83.1 us -> 16.1 us  [gather_smalls(): full = lax.all_gather(packed, 'fsdp', axis=0, tiled=True)]
    ppermute x0 -> x16, waiting for transfers between devices: none -> 43.5 us  [swap_sum(): other = lax.ppermute(part, 'ctx', [(i, i ^ bit) for i in range(size)])]
    all_gather x6 -> x5, waiting for transfers between devices: 215 us -> 255 us  [the longest x1 80.2 us: local(): full_in_weight = lax.all_gather(in_weight, 'fsdp', axis=0, tiled=True)]
    unnamed x13 -> x11, waiting for transfers between devices: 2.41 us -> 38.5 us
    unnamed x1 -> x0, blocking collectives: 26.4 us -> none
    ppermute x0 -> x16, starting transfers between devices: none -> 19.5 us  [swap_sum(): other = lax.ppermute(part, 'ctx', [(i, i ^ bit) for i in range(size)])]
  transfers between devices with their start and end apart: 13 -> 26, of which waited for: 9 -> 21; matrix products, arithmetic and copies ran while one was open for 13% -> 25% of each run, Pallas kernels for 0% -> 0%
where the time goes in v1:
time: 739 us; the launch traced here: 734 us
  waiting for transfers between devices  456 us (62%)
  matrix products  162 us (22%)
  local copies, waits for them, and re-layouts  37.1 us (5%)
  other arithmetic  26.8 us (4%)
  starting transfers between devices  20.3 us (3%)
  blocking collectives  16.1 us (2%)
  between operations  15.6 us (2%)
    reduce_scatter x3, waiting for transfers between devices, scatter_half(): lax.psum_scatter(grad.astype(jnp.bfloat16), 'fsdp', scatter_dimension=0,...  104 us
    dot_general x6, matrix products, mix(): jnp.einsum(pattern, left_op, right_op, preferred_element_type=jnp.float32)  98.6 us
    all_gather x1, waiting for transfers between devices, local(): full_in_weight = lax.all_gather(in_weight, 'fsdp', axis=0, tiled=True)  80.2 us
    all_gather x1, waiting for transfers between devices, local(): full_down_weight = lax.all_gather(down_weight, 'fsdp', axis=0, tiled=True)  73.2 us
    all_gather x1, waiting for transfers between devices, local(): lax.all_gather(jnp.concatenate([keys_local, values_local], axis=1).reshap...  48.2 us
    all_gather x1, waiting for transfers between devices, local(): full_qkv = lax.all_gather(qkv_weight, 'fsdp', axis=0, tiled=True)  46.5 us
    ppermute x16, waiting for transfers between devices, swap_sum(): other = lax.ppermute(part, 'ctx', [(i, i ^ bit) for i in range(size)])  43.5 us
    unnamed x11, waiting for transfers between devices  38.5 us
  transfers between devices with their start and end apart: 26, of which 21 were waited for; matrix products, arithmetic and copies ran while one was open for 25% of the time, Pallas kernels for 0%

profile of v1, /device:TPU:0, one launch (start us, length us, event | category | flops | bytes accessed | tf_op | source)
XLA Modules:
  0.0 734.3 jit_solution(15374058771902463985)
XLA Ops:
  14.7 16.1 %all-gather.2 = bf16[8,1,1536]{2,1,0:T(2,128)(2,1)S(1)} all-gather(bf16[1,1,1536]{2,1,0:T(2,128)(2,1)S(1)} %reshape.360), channel_id=2, replica_groups=mesh['ctx'=4,'fsdp'=8] {'fsdp'}, dimensions={0}, use_global_device_ids=true | all-gather | bytes 27648 | tf_op jit(solution)/shard_map/all_gather | solution.py:125
  30.8 46.5 %all-gather.9.cloned.1.call-done = bf16[1024,3072]{1,0:T(8,128)(2,1)} async-done(((bf16[128,3072]{1,0:T(8,128)(2,1)}), bf16[1024,3072]{1,0:T(8,128)(2,1)}) %all-gather.9.cloned.1.call-update) | async-done | bytes 6291472 | tf_op jit(solution)/shard_map/all_gather | solution.py:194
  77.3 4.8 fusion.57
  86.7 48.2 %all-gather.17.cloned.1.call-done = bf16[1024,2048]{1,0:T(8,128)(2,1)} async-done(((bf16[256,2048]{1,0:T(8,128)(2,1)}), bf16[1024,2048]{1,0:T(8,128)(2,1)}) %all-gather.17.cloned.1.call-update) | async-done | bytes 4194320 | tf_op jit(solution)/shard_map/all_gather | solution.py:200
  144.3 4.9 fusion.4
  149.2 4.1 exponential_reduce_fusion
  154.9 4.2 convolution_convert_fusion.4
  159.1 6.5 all-gather.11.cloned.1.call-done
  168.3 80.2 %all-gather.13.cloned.1.call-done = bf16[1024,4096]{1,0:T(8,128)(2,1)} async-done(((bf16[128,4096]{1,0:T(8,128)(2,1)}), bf16[1024,4096]{1,0:T(8,128)(2,1)}) %all-gather.13.cloned.1.call-update) | async-done | bytes 8388624 | tf_op jit(solution)/shard_map/all_gather | solution.py:196
  248.6 8.8 %multiply_convert_fusion.1 = (bf16[256,4096]{1,0:T(8,128)(2,1)}, f32[256,4096]{1,0:T(8,128)}) fusion(f32[4096]{0:T(1024)S(1)} %bitcast.162, bf16[1024,4096]{1,0:T(8,128)(2,1)} %all-gather.13.cloned.1.call-done, f32[256,1024]{1,0:T(8,128)S(1)} %get-tuple-element.173, f32[1024]{0:T(1024)S(1)} %get-tuple-element.165, f32[1024]{0:T(1024)S(1)} %get-tuple-element.166, ...), kind=kOutput, calls=%fused_computation.30 | convolution fusion | flops 2155085824 | bytes 15755264 | tf_op jit(solution)/shard_map/dot_general | solution.py:219
  257.4 73.2 %all-gather.15.cloned.1.call-done = bf16[4096,1024]{1,0:T(8,128)(2,1)} async-done(((bf16[512,1024]{1,0:T(8,128)(2,1)}), bf16[4096,1024]{1,0:T(8,128)(2,1)}) %all-gather.15.cloned.1.call-update) | async-done | bytes 8388624 | tf_op jit(solution)/shard_map/all_gather | solution.py:197
  330.6 6.5 fusion.101
  339.2 5.6 convolution_convert_fusion
  344.9 7.6 %fusion.104 = (bf16[4096]{0:T(1024)(128)(2,1)S(1)}, bf16[256,4096]{1,0:T(8,128)(2,1)S(1)}) fusion(f32[256,4096]{1,0:T(8,128)} %get-tuple-element.175, bf16[4096,1024]{1,0:T(8,128)(2,1)} %all-gather.15.cloned.1.call-done, f32[256,1024]{1,0:T(8,128)S(1)} %get-tuple-element.127), kind=kOutput, calls=%fused_computation.170 | convolution fusion | flops 2159276032 | bytes 15736832 | tf_op jit(solution)/shard_map/dot_general | solution.py:30
  352.5 6.9 multiply_reduce_fusion.1
  361.5 10.0 %fusion.105 = f32[16,256,1024]{2,1,0:T(8,128)} fusion(bf16[256,16,64]{0,2,1:T(8,128)(2,1)} %bitcast.148, bf16[1024,16,64]{0,2,1:T(8,128)(2,1)} %bitcast.140), kind=kOutput, calls=%fused_computation.171 | convolution fusion | flops 536870912 | bytes 19398656 | tf_op jit(solution)/shard_map/while/body/eval_jaxpr/qhd,khd->hqk/dot_general | solution.py:20
  371.5 38.8 %fusion.32 = bf16[16,64,1024]{2,1,0:T(8,128)(2,1)} fusion(bf16[256,16,64]{0,2,1:T(8,128)(2,1)S(1)} %bitcast.147, f32[16,256,1024]{2,1,0:T(8,128)} %fusion.105, f32[16,256,1024]{2,1,0:T(8,128)} %copy-done, f32[16,256]{1,0:T(8,128)S(1)} %log_add_fusion, pred[1024]{0:T(1024)(128)(4,1)S(1)} %fusion.65), kind=kOutput, calls=%fused_computation.36 | convolution fusion | flops 584061952 | bytes 36193280 | tf_op jit(solution)/shard_map/while/body/eval_jaxpr/hqk,qhd->khd/dot_general | solution.py:20
  410.3 9.8 %convolution_convert_fusion.2 = bf16[16,64,1024]{2,1,0:T(8,128)(2,1)S(1)} fusion(bf16[256,16,64]{0,2,1:T(8,128)(2,1)} %bitcast.149, f32[16,256,1024]{2,1,0:T(8,128)} %copy-done, f32[16,256]{1,0:T(8,128)S(1)} %log_add_fusion, pred[1024]{0:T(1024)(128)(4,1)S(1)} %fusion.65), kind=kOutput, calls=%fused_computation.35 | convolution fusion | flops 554696704 | bytes 19416064 | tf_op jit(solution)/shard_map/while/body/eval_jaxpr/hqk,qhd->khd/dot_general | solution.py:20
  422.4 10.6 %reduce-scatter.8.cloned.1.call-done = bf16[512,1024]{1,0:T(8,128)(2,1)} async-done(((bf16[4096,1024]{1,0:T(8,128)(2,1)}), bf16[512,1024]{1,0:T(8,128)(2,1)}) %reduce-scatter.8.cloned.1.call-update) | async-done | bytes 1048592 | tf_op jit(solution)/shard_map/reduce_scatter | solution.py:135
  433.1 31.0 %fusion.96 = (bf16[16,64]{1,0:T(8,128)(2,1)S(1)}, bf16[256,16,64]{0,2,1:T(8,128)(2,1)}) fusion(bf16[1024,16,64]{0,2,1:T(8,128)(2,1)} %bitcast.142, f32[16,256,1024]{2,1,0:T(8,128)} %fusion.105, f32[16,256,1024]{2,1,0:T(8,128)} %copy-done, f32[16,256]{1,0:T(8,128)S(1)} %log_add_fusion, pred[1024]{0:T(1024)(128)(4,1)S(1)} %fusion.65), kind=kOutput, calls=%fused_computation.164 | convolution fusion | flops 583536640 | bytes 36195328 | tf_op jit(solution)/shard_map/while/body/eval_jaxpr/hqk,khd->qhd/dot_general | solution.py:20
  464.1 7.4 %convolution_convert_fusion.1 = bf16[1024,4096]{1,0:T(8,128)(2,1)} fusion(bf16[256,4096]{1,0:T(8,128)(2,1)} %copy-done.8, f32[256,1024]{1,0:T(8,128)S(1)} %get-tuple-element.173, f32[1024]{0:T(1024)S(1)} %get-tuple-element.165, f32[1024]{0:T(1024)S(1)} %get-tuple-element.166, f32[256]{0:T(256)S(1)} %add_rsqrt_fusion.1, f32[256]{0:T(256)S(1)} %broadcast_multiply_fusion.5), kind=kOutput, calls=%fused_computation.20 | convolution fusion | flops 2152988672 | bytes 11544576 | tf_op jit(solution)/shard_map/dot_general | solution.py:24
  471.5 15.6 %reduce-scatter.10.cloned.1.call-done = bf16[1,256,2048]{1,2,0:T(8,128)(2,1)} async-done(((bf16[1,1024,2048]{1,2,0:T(8,128)(2,1)}), bf16[1,256,2048]{1,2,0:T(8,128)(2,1)}) %reduce-scatter.10.cloned.1.call-update) | async-done | bytes 1048592 | tf_op jit(solution)/shard_map/reduce_scatter | solution.py:259
  488.5 5.8 convert_bitcast_fusion
  494.3 8.5 %copy.63 = bf16[1024,3072]{1,0:T(8,128)(2,1)} copy(bf16[1024,3072]{0,1:T(8,128)(2,1)} %convert_bitcast_fusion) | data formatting | bytes 12582912
  506.2 11.5 %collective-permute-done.12 = bf16[256,1024]{1,0:T(8,128)(2,1)S(1)} collective-permute-done((bf16[256,1024]{1,0:T(8,128)(2,1)S(1)}, bf16[256,1024]{1,0:T(8,128)(2,1)S(1)}, u32[]{:S(2)}, u32[]{:S(2)}) %collective-permute-start.12) | collective-permute-done | bytes 524320 | tf_op jit(solution)/shard_map/ppermute | solution.py:147
  524.3 8.8 %collective-permute-done.13 = bf16[256,1024]{1,0:T(8,128)(2,1)} collective-permute-done((bf16[256,1024]{1,0:T(8,128)(2,1)}, bf16[256,1024]{1,0:T(8,128)(2,1)}, u32[]{:S(2)}, u32[]{:S(2)}) %collective-permute-start.13) | collective-permute-done | bytes 524320 | tf_op jit(solution)/shard_map/ppermute | solution.py:147
  537.5 35.3 %reduce-scatter.16.cloned.1.call-done = bf16[128,3072]{1,0:T(8,128)(2,1)} async-done(((bf16[1024,3072]{1,0:T(8,128)(2,1)}), bf16[128,3072]{1,0:T(8,128)(2,1)}) %reduce-scatter.16.cloned.1.call-update) | async-done | bytes 786448
  588.8 5.6 fusion.44
  595.4 6.8 collective-permute-done.3
  602.2 60.8 %reduce-scatter.14.cloned.1.call-done = bf16[128,4096]{1,0:T(8,128)(2,1)} async-done(((bf16[1024,4096]{1,0:T(8,128)(2,1)}), bf16[128,4096]{1,0:T(8,128)(2,1)}) %reduce-scatter.14.cloned.1.call-update) | async-done | bytes 1048592 | tf_op jit(solution)/shard_map/reduce_scatter | solution.py:135
  668.4 32.4 %reduce-scatter.12.cloned.1.call-done = bf16[144,1024]{1,0:T(8,128)(2,1)} async-done(((bf16[1152,1024]{1,0:T(8,128)(2,1)}), bf16[144,1024]{1,0:T(8,128)(2,1)}) %reduce-scatter.12.cloned.1.call-update) | async-done | bytes 294928 | tf_op jit(solution)/shard_map/reduce_scatter | solution.py:135
  717.5 6.6 collective-permute-done.7
  (180 shorter events, 89.5 us)
Async XLA Ops:
  7.2 70.1 %all-gather.9.cloned.1.call-start = ((), (), s32[]{:S(2)}) async-start(), calls=%async_computation.5 | async-start | bytes 7077888 | tf_op jit(solution)/shard_map/all_gather | solution.py:194
  7.9 126.9 %all-gather.17.cloned.1.call-start = ((), (), s32[]{:S(2)}) async-start(), calls=%async_computation.13 | async-start | bytes 5242880 | tf_op jit(solution)/shard_map/all_gather | solution.py:200
  83.5 82.1 %all-gather.11.cloned.1.call-start = ((), (), s32[]{:S(2)}) async-start(), calls=%async_computation.6 | async-start | bytes 2359296 | tf_op jit(solution)/shard_map/all_gather | solution.py:195
  84.2 164.3 %all-gather.13.cloned.1.call-start = ((), (), s32[]{:S(2)}) async-start(), calls=%async_computation.7 | async-start | bytes 9437184 | tf_op jit(solution)/shard_map/all_gather | solution.py:196
  84.8 245.7 %all-gather.15.cloned.1.call-start = ((), (), s32[]{:S(2)}) async-start(), calls=%async_computation.8 | async-start | bytes 9437184 | tf_op jit(solution)/shard_map/all_gather | solution.py:197
  85.4 347.6 %reduce-scatter.8.cloned.1.call-start = ((), (), s32[]{:S(2)}) async-start(), calls=%async_computation.9 | async-start | bytes 9437184 | tf_op jit(solution)/shard_map/reduce_scatter | solution.py:135
  86.6 57.6 %copy-start.10 = (bf16[256,1024]{0,1:T(8,128)(2,1)}, bf16[256,1024]{0,1:T(8,128)(2,1)S(1)}, u32[]{:S(2)}) copy-start(bf16[256,1024]{0,1:T(8,128)(2,1)S(1)} %copy.58) | copy-start | bytes 1572868
  154.9 10.7 %copy-start.14 = (bf16[1,256,1024]{2,1,0:T(8,128)(2,1)S(1)}, bf16[1,256,1024]{2,1,0:T(8,128)(2,1)}, u32[]{:S(2)}) copy-start(bf16[1,256,1024]{2,1,0:T(8,128)(2,1)} %param.16) | copy-start | bytes 1572868
  159.1 98.3 %copy-start.9 = (bf16[16,64,256]{2,1,0:T(8,128)(2,1)}, bf16[16,64,256]{2,1,0:T(8,128)(2,1)S(1)}, u32[]{:S(2)}) copy-start(bf16[16,64,256]{2,1,0:T(8,128)(2,1)S(1)} %convolution_convert_fusion.4) | copy-start | bytes 1572868
  344.8 142.2 %reduce-scatter.10.cloned.1.call-start = ((), (), s32[]{:S(2)}) async-start(), calls=%async_computation.10 | async-start | bytes 5242880 | tf_op jit(solution)/shard_map/reduce_scatter | solution.py:259
  433.0 139.7 %reduce-scatter.16.cloned.1.call-start = ((), (), s32[]{:S(2)}) async-start(), calls=%async_computation.14 | async-start | bytes 7077888
  464.1 24.4 %copy-start.15 = (bf16[1,256,1024]{2,1,0:T(8,128)(2,1)S(1)}, bf16[1,256,1024]{2,1,0:T(8,128)(2,1)}, u32[]{:S(2)}) copy-start(bf16[1,256,1024]{2,1,0:T(8,128)(2,1)} %param.16) | copy-start | bytes 1572868
  502.9 160.2 %reduce-scatter.14.cloned.1.call-start = ((), (), s32[]{:S(2)}) async-start(), calls=%async_computation.12 | async-start | bytes 9437184 | tf_op jit(solution)/shard_map/reduce_scatter | solution.py:135
  503.6 197.2 %reduce-scatter.12.cloned.1.call-start = ((), (), s32[]{:S(2)}) async-start(), calls=%async_computation.11 | async-start | bytes 2654208 | tf_op jit(solution)/shard_map/reduce_scatter | solution.py:135
  504.2 13.6 %collective-permute-start.12 = (bf16[256,1024]{1,0:T(8,128)(2,1)S(1)}, bf16[256,1024]{1,0:T(8,128)(2,1)S(1)}, u32[]{:S(2)}, u32[]{:S(2)}) collective-permute-start(bf16[256,1024]{1,0:T(8,128)(2,1)S(1)} %get-tuple-element.137), channel_id=1, source_target_pairs={{0,8},{8,0},{16,24},{24,16},{1,9},{9,1},{17,25},{25,17},{2,10},{10... | collective-permute-start | bytes 1572872 | tf_op jit(solution)/shard_map/ppermute | solution.py:147
  505.7 13.2 %collective-permute-start.14 = (bf16[256,1024]{1,0:T(8,128)(2,1)S(1)}, bf16[256,1024]{1,0:T(8,128)(2,1)S(1)}, u32[]{:S(2)}, u32[]{:S(2)}) collective-permute-start(bf16[256,1024]{1,0:T(8,128)(2,1)S(1)} %get-tuple-element.138), channel_id=1, source_target_pairs={{0,16},{8,24},{16,0},{24,8},{1,17},{9,25},{17,1},{25,9},{2,18},{10... | collective-permute-start | bytes 1572872 | tf_op jit(solution)/shard_map/ppermute | solution.py:147
  520.3 12.8 %collective-permute-start.13 = (bf16[256,1024]{1,0:T(8,128)(2,1)}, bf16[256,1024]{1,0:T(8,128)(2,1)}, u32[]{:S(2)}, u32[]{:S(2)}) collective-permute-start(bf16[256,1024]{1,0:T(8,128)(2,1)} %get-tuple-element.135), channel_id=1, source_target_pairs={{0,16},{8,24},{16,0},{24,8},{1,17},{9,25},{17,1},{25,9},{2,18},{10... | collective-permute-start | bytes 1572872 | tf_op jit(solution)/shard_map/ppermute | solution.py:147
  522.8 56.9 %collective-permute-start.15 = (bf16[256,1024]{1,0:T(8,128)(2,1)}, bf16[256,1024]{1,0:T(8,128)(2,1)}, u32[]{:S(2)}, u32[]{:S(2)}) collective-permute-start(bf16[256,1024]{1,0:T(8,128)(2,1)} %get-tuple-element.136), channel_id=1, source_target_pairs={{0,8},{8,0},{16,24},{24,16},{1,9},{9,1},{17,25},{25,17},{2,10},{10... | collective-permute-start | bytes 1572872 | tf_op jit(solution)/shard_map/ppermute | solution.py:147
  537.5 42.2 %copy-start.13 = (bf16[256,1024]{1,0:T(8,128)(2,1)S(1)}, bf16[256,1024]{1,0:T(8,128)(2,1)}, u32[]{:S(2)}) copy-start(bf16[256,1024]{1,0:T(8,128)(2,1)} %get-tuple-element.136) | copy-start | bytes 1572868
  576.6 9.0 %collective-permute-start = (bf16[64,3072]{1,0:T(8,128)(2,1)S(1)}, bf16[64,3072]{1,0:T(8,128)(2,1)S(1)}, u32[]{:S(2)}, u32[]{:S(2)}) collective-permute-start(bf16[64,3072]{1,0:T(8,128)(2,1)S(1)} %get-tuple-element.150), channel_id=1, source_target_pairs={{0,8},{8,0},{16,24},{24,16},{1,9},{9,1},{17,25},{25,17},{2,10},{10... | collective-permute-start | bytes 1179656 | tf_op jit(solution)/shard_map/ppermute | solution.py:147
  578.2 8.9 %collective-permute-start.2 = (bf16[64,3072]{1,0:T(8,128)(2,1)S(1)}, bf16[64,3072]{1,0:T(8,128)(2,1)S(1)}, u32[]{:S(2)}, u32[]{:S(2)}) collective-permute-start(bf16[64,3072]{1,0:T(8,128)(2,1)S(1)} %get-tuple-element.151), channel_id=1, source_target_pairs={{0,16},{8,24},{16,0},{24,8},{1,17},{9,25},{17,1},{25,9},{2,18},{10... | collective-permute-start | bytes 1179656 | tf_op jit(solution)/shard_map/ppermute | solution.py:147
  587.3 8.0 %collective-permute-start.1 = (bf16[64,3072]{1,0:T(8,128)(2,1)S(1)}, bf16[64,3072]{1,0:T(8,128)(2,1)S(1)}, u32[]{:S(2)}, u32[]{:S(2)}) collective-permute-start(bf16[64,3072]{1,0:T(8,128)(2,1)S(1)} %get-tuple-element.148), channel_id=1, source_target_pairs={{0,16},{8,24},{16,0},{24,8},{1,17},{9,25},{17,1},{25,9},{2,18},{10... | collective-permute-start | bytes 1179656 | tf_op jit(solution)/shard_map/ppermute | solution.py:147
  594.4 7.8 %collective-permute-start.3 = (bf16[64,3072]{1,0:T(8,128)(2,1)S(1)}, bf16[64,3072]{1,0:T(8,128)(2,1)S(1)}, u32[]{:S(2)}, u32[]{:S(2)}) collective-permute-start(bf16[64,3072]{1,0:T(8,128)(2,1)S(1)} %get-tuple-element.149), channel_id=1, source_target_pairs={{0,8},{8,0},{16,24},{24,16},{1,9},{9,1},{17,25},{25,17},{2,10},{10... | collective-permute-start | bytes 1179656 | tf_op jit(solution)/shard_map/ppermute | solution.py:147
  663.1 47.1 %copy-start.4 = (bf16[128,4096]{1,0:T(8,128)(2,1)S(1)}, bf16[128,4096]{1,0:T(8,128)(2,1)}, u32[]{:S(2)}) copy-start(bf16[128,4096]{1,0:T(8,128)(2,1)} %reduce-scatter.14.cloned.1.call-done) | copy-start | bytes 3145732
  665.4 44.7 %collective-permute-start.8 = (bf16[64,4096]{1,0:T(8,128)(2,1)}, bf16[64,4096]{1,0:T(8,128)(2,1)S(1)}, u32[]{:S(2)}, u32[]{:S(2)}) collective-permute-start(bf16[64,4096]{1,0:T(8,128)(2,1)} %get-tuple-element.141), channel_id=1, source_target_pairs={{0,8},{8,0},{16,24},{24,16},{1,9},{9,1},{17,25},{25,17},{2,10},{10... | collective-permute-start | bytes 1572872 | tf_op jit(solution)/shard_map/ppermute | solution.py:147
  666.9 43.3 %collective-permute-start.10 = (bf16[64,4096]{1,0:T(8,128)(2,1)}, bf16[64,4096]{1,0:T(8,128)(2,1)}, u32[]{:S(2)}, u32[]{:S(2)}) collective-permute-start(bf16[64,4096]{1,0:T(8,128)(2,1)} %get-tuple-element.142), channel_id=1, source_target_pairs={{0,16},{8,24},{16,0},{24,8},{1,17},{9,25},{17,1},{25,9},{2,18},{10... | collective-permute-start | bytes 1572872 | tf_op jit(solution)/shard_map/ppermute | solution.py:147
  701.8 5.2 collective-permute-start.6
  703.3 5.1 collective-permute-start.4
  709.5 6.8 collective-permute-start.5
  711.5 14.1 %collective-permute-start.9 = (bf16[64,4096]{1,0:T(8,128)(2,1)S(1)}, bf16[64,4096]{1,0:T(8,128)(2,1)S(1)}, u32[]{:S(2)}, u32[]{:S(2)}) collective-permute-start(bf16[64,4096]{1,0:T(8,128)(2,1)S(1)} %get-tuple-element.139), channel_id=1, source_target_pairs={{0,16},{8,24},{16,0},{24,8},{1,17},{9,25},{17,1},{25,9},{2,18},{10... | collective-permute-start | bytes 1572872 | tf_op jit(solution)/shard_map/ppermute | solution.py:147
  713.1 12.5 %collective-permute-start.11 = (bf16[64,4096]{1,0:T(8,128)(2,1)S(1)}, bf16[64,4096]{1,0:T(8,128)(2,1)S(1)}, u32[]{:S(2)}, u32[]{:S(2)}) collective-permute-start(bf16[64,4096]{1,0:T(8,128)(2,1)S(1)} %get-tuple-element.140), channel_id=1, source_target_pairs={{0,8},{8,0},{16,24},{24,16},{1,9},{9,1},{17,25},{25,17},{2,10},{10... | collective-permute-start | bytes 1572872 | tf_op jit(solution)/shard_map/ppermute | solution.py:147
  714.5 9.6 %collective-permute-start.7 = (bf16[72,1024]{1,0:T(8,128)(2,1)S(1)}, bf16[72,1024]{1,0:T(8,128)(2,1)S(1)}, u32[]{:S(2)}, u32[]{:S(2)}) collective-permute-start(bf16[72,1024]{1,0:T(8,128)(2,1)S(1)} %get-tuple-element.152), channel_id=1, source_target_pairs={{0,16},{8,24},{16,0},{24,8},{1,17},{9,25},{17,1},{25,9},{2,18},{10... | collective-permute-start | bytes 442376 | tf_op jit(solution)/shard_map/ppermute | solution.py:147
  (16 other events, 112.6 us)
Sparse Core Ops, SparseCore 0:
  9.6 67.6 all-gather.8
  83.6 51.1 all-gather.16
  136.5 29.1 all-gather.10
  167.1 81.4 all-gather.12
  250.0 80.5 all-gather.14
  345.0 88.0 reduce-scatter.7
  436.0 51.0 reduce-scatter.9
  503.0 69.7 reduce-scatter.15
  575.0 87.9 reduce-scatter.13
  665.2 35.5 reduce-scatter.11
